TPU v7x, 32 devices: a whole 2x2x4 slice. The times are simulated.
32 devices in a mesh: dp: 8 (over z, x), tensor: 4 (over y, core).
Axes of the slice: x: 2, y: 2, z: 4, core: 2. Of those that a mesh axis runs over, the one named last changes fastest.
Arguments:
- hidden_in: bfloat16 [4096, 1024], P(('dp', 'tensor')), may hold values from -8 to 8
- cotangent: bfloat16 [4096, 1024], P(('dp', 'tensor')), may hold values from -6 to 6
- lengths: int32 [8], P('dp'), may hold values from 128 to 512, as said below
- query_weight: bfloat16 [1024, 1024], P('dp', 'tensor'), as said below
- key_weight: bfloat16 [1024, 1024], P('dp', 'tensor'), as said below
- value_weight: bfloat16 [1024, 1024], P('dp', 'tensor'), may hold values from -0.1875 to 0.1875
- output_weight: bfloat16 [1024, 1024], P('tensor', 'dp'), may hold values from -1 to 1
- up_weight: bfloat16 [1024, 4096], P('dp', 'tensor'), may hold values from -0.1875 to 0.1875
- down_weight: bfloat16 [4096, 1024], P('tensor', 'dp'), may hold values from -0.09375 to 0.09375
- query_bias: float32 [1024], P('tensor'), may hold values from -3 to 3
- value_bias: float32 [1024], P('tensor'), may hold values from -3 to 3
- output_bias: float32 [1024], replicated, may hold values from -3 to 3
- up_bias: float32 [4096], P('tensor'), may hold values from -3 to 3
- down_bias: float32 [1024], replicated, may hold values from -3 to 3
- first_gain: float32 [1024], replicated, may hold values from 0.5 to 1.5
- first_shift: float32 [1024], replicated, may hold values from -3 to 3
- second_gain: float32 [1024], replicated, may hold values from 0.5 to 1.5
- second_shift: float32 [1024], replicated, may hold values from -3 to 3
Outputs:
- hidden_out: bfloat16 [4096, 1024], P(('dp', 'tensor'))
- grad_in: bfloat16 [4096, 1024], P(('dp', 'tensor'))
- grad_query_weight: float32 [1024, 1024], P('dp', 'tensor')
- grad_key_weight: float32 [1024, 1024], P('dp', 'tensor')
- grad_value_weight: float32 [1024, 1024], P('dp', 'tensor')
- grad_output_weight: float32 [1024, 1024], P('tensor', 'dp')
- grad_up_weight: float32 [1024, 4096], P('dp', 'tensor')
- grad_down_weight: float32 [4096, 1024], P('tensor', 'dp')
- grad_query_bias: float32 [1024], P('tensor')
- grad_value_bias: float32 [1024], P('tensor')
- grad_output_bias: float32 [1024], replicated
- grad_up_bias: float32 [4096], P('tensor')
- grad_down_bias: float32 [1024], replicated
- grad_first_gain: float32 [1024], replicated
- grad_first_shift: float32 [1024], replicated
- grad_second_gain: float32 [1024], replicated
- grad_second_shift: float32 [1024], replicated
Inputs may be any that keep to these rules, and one draw needn't show every extreme that they name: `lengths`: positions of a sequence at or past its entry are padding keys. Some sequence is full. `query_weight`: A projection scaled by its fan-in. `key_weight`: A projection scaled by its fan-in.
All inputs are finite; a program needn't handle non-finite values.
Results may differ from a plain program's by a relative error of at most 0.02.
Values may be sent and summed in bfloat16 or wider, within the bound.
No kernel may reach another device: no remote copies, remote signals or barrier semaphores. Data moves between devices by JAX's collectives and lax.ppermute only.
A program may use at most 128 MiB of HBM per device.

v0:
```python
import jax
import jax.numpy as jnp
from jax import lax
from jax.sharding import PartitionSpec as P

HD = 64
EPSILON = 1e-12
ROOT_HALF = 0.7071067811865476
INV_ROOT_TWO_PI = 0.3989422804014327
MASKED = -1e30


def matmul(left_side, right_side):
    return jnp.dot(left_side, right_side, preferred_element_type=jnp.float32)


def matmul_nt(left_side, right_side):
    return lax.dot_general(
        left_side, right_side, (((1,), (1,)), ((), ())), preferred_element_type=jnp.float32
    )


def matmul_tn(left_side, right_side):
    return lax.dot_general(
        left_side, right_side, (((0,), (0,)), ((), ())), preferred_element_type=jnp.float32
    )


def gelu_value(pre_act):
    return pre_act * 0.5 * (1.0 + lax.erf(pre_act * ROOT_HALF))


def gelu_slope(pre_act):
    cumulative = 0.5 * (1.0 + lax.erf(pre_act * ROOT_HALF))
    density = jnp.exp(-0.5 * pre_act * pre_act) * INV_ROOT_TWO_PI
    return cumulative + pre_act * density


def norm_forward(summed, gain_vector, shift_vector):
    centre = summed - jnp.mean(summed, axis=-1, keepdims=True)
    spread = jnp.mean(centre * centre, axis=-1, keepdims=True)
    inverse = lax.rsqrt(spread + EPSILON)
    normed = centre * inverse
    return (normed * gain_vector + shift_vector, normed, inverse)


def norm_backward(upstream, gain_vector, normed, inverse):
    scaled = upstream * gain_vector
    return inverse * (
        scaled
        - jnp.mean(scaled, axis=-1, keepdims=True)
        - normed * jnp.mean(scaled * normed, axis=-1, keepdims=True)
    )


def fetch_weights(query_weight, key_weight, value_weight, up_weight, output_weight, down_weight):
    row_parts = (
        lax.all_gather(query_weight, "dp", axis=0, tiled=True),
        lax.all_gather(key_weight, "dp", axis=0, tiled=True),
        lax.all_gather(value_weight, "dp", axis=0, tiled=True),
        lax.all_gather(up_weight, "dp", axis=0, tiled=True),
    )
    col_parts = (
        lax.all_gather(output_weight, "dp", axis=1, tiled=True),
        lax.all_gather(down_weight, "dp", axis=1, tiled=True),
    )
    return (row_parts, col_parts)


def masked_scores(query_block, key_heads, key_valid, score_scale):
    scores = (
        jnp.einsum("qhd,khd->hqk", query_block, key_heads, preferred_element_type=jnp.float32)
        * score_scale
    )
    return jnp.where(key_valid[None, None, :], scores, MASKED)


def widen(vector, tensor_index, n_tensor):
    zeros_full = jnp.zeros((n_tensor * vector.shape[0],), jnp.float32)
    return lax.dynamic_update_slice_in_dim(zeros_full, vector, tensor_index * vector.shape[0], 0)


def shards(
    hidden_in,
    cotangent,
    lengths,
    query_weight,
    key_weight,
    value_weight,
    output_weight,
    up_weight,
    down_weight,
    query_bias,
    value_bias,
    output_bias,
    up_bias,
    down_bias,
    first_gain,
    first_shift,
    second_gain,
    second_shift,
):
    n_tensor = lax.axis_size("tensor")
    tensor_index = lax.axis_index("tensor")
    local_rows = hidden_in.shape[0]
    seq_len = local_rows * n_tensor
    local_width = query_weight.shape[1]
    local_heads = local_width // HD
    score_scale = HD ** (-0.5)
    length = lengths[0]
    key_valid = jnp.arange(seq_len, dtype=jnp.int32) < length
    row_parts, col_parts = fetch_weights(
        query_weight, key_weight, value_weight, up_weight, output_weight, down_weight
    )
    query_full, key_full, value_full, up_full = row_parts
    output_full, down_full = col_parts
    hidden_full = lax.all_gather(hidden_in, "tensor", axis=0, tiled=True)
    queries = (matmul(hidden_full, query_full) + query_bias).astype(jnp.bfloat16)
    key_rows = matmul(hidden_full, key_full).astype(jnp.bfloat16)
    value_rows = (matmul(hidden_full, value_full) + value_bias).astype(jnp.bfloat16)
    query_heads = queries.reshape(seq_len, local_heads, HD)
    key_heads = key_rows.reshape(seq_len, local_heads, HD)
    value_heads = value_rows.reshape(seq_len, local_heads, HD)
    scores = masked_scores(query_heads, key_heads, key_valid, score_scale)
    row_peak = jnp.max(scores, axis=-1, keepdims=True)
    log_total = row_peak + jnp.log(jnp.sum(jnp.exp(scores - row_peak), axis=-1, keepdims=True))
    probs_low = jnp.exp(scores - log_total).astype(jnp.bfloat16)
    context_block = jnp.einsum(
        "hqk,khd->qhd", probs_low, value_heads, preferred_element_type=jnp.float32
    )
    context_parts = context_block.astype(jnp.bfloat16)
    context = context_parts.reshape(seq_len, local_width)
    attn_rows = lax.psum_scatter(
        matmul(context, output_full).astype(jnp.bfloat16), "tensor", scatter_dimension=0, tiled=True
    ).astype(jnp.float32)
    first_sum = hidden_in.astype(jnp.float32) + attn_rows + output_bias
    first_out, first_normed, first_inverse = norm_forward(first_sum, first_gain, first_shift)
    first_low = first_out.astype(jnp.bfloat16)
    normed_full = lax.all_gather(first_low, "tensor", axis=0, tiled=True)
    pre_act = matmul(normed_full, up_full) + up_bias
    activated = gelu_value(pre_act).astype(jnp.bfloat16)
    mlp_rows = lax.psum_scatter(
        matmul(activated, down_full).astype(jnp.bfloat16), "tensor", scatter_dimension=0, tiled=True
    ).astype(jnp.float32)
    second_sum = first_out + mlp_rows + down_bias
    second_out, second_normed, second_inverse = norm_forward(second_sum, second_gain, second_shift)
    hidden_out = second_out.astype(jnp.bfloat16)
    upstream = cotangent.astype(jnp.float32)
    grad_second_gain = jnp.sum(upstream * second_normed, axis=0)
    grad_second_shift = jnp.sum(upstream, axis=0)
    second_grad = norm_backward(upstream, second_gain, second_normed, second_inverse)
    grad_down_bias = jnp.sum(second_grad, axis=0)
    second_low = second_grad.astype(jnp.bfloat16)
    second_full = lax.all_gather(second_low, "tensor", axis=0, tiled=True)
    grad_down = matmul_tn(activated, second_full)
    pre_grad = matmul_nt(second_full, down_full) * gelu_slope(pre_act)
    grad_up_bias = jnp.sum(pre_grad, axis=0)
    pre_low = pre_grad.astype(jnp.bfloat16)
    grad_up = matmul_tn(normed_full, pre_low)
    first_grad_in = second_grad + lax.psum_scatter(
        matmul_nt(pre_low, up_full).astype(jnp.bfloat16), "tensor", scatter_dimension=0, tiled=True
    ).astype(jnp.float32)
    grad_first_gain = jnp.sum(first_grad_in * first_normed, axis=0)
    grad_first_shift = jnp.sum(first_grad_in, axis=0)
    first_grad = norm_backward(first_grad_in, first_gain, first_normed, first_inverse)
    grad_output_bias = jnp.sum(first_grad, axis=0)
    first_grad_low = first_grad.astype(jnp.bfloat16)
    attn_grad_full = lax.all_gather(first_grad_low, "tensor", axis=0, tiled=True)
    grad_output = matmul_tn(context, attn_grad_full)
    context_grad = matmul_nt(attn_grad_full, output_full).astype(jnp.bfloat16)
    grad_heads = context_grad.reshape(seq_len, local_heads, HD)
    scores = masked_scores(query_heads, key_heads, key_valid, score_scale)
    attn_probs = jnp.exp(scores - log_total)
    probs_low = attn_probs.astype(jnp.bfloat16)
    prob_grad = jnp.einsum(
        "qhd,khd->hqk", grad_heads, value_heads, preferred_element_type=jnp.float32
    )
    row_inner = jnp.sum(attn_probs * prob_grad, axis=-1, keepdims=True)
    score_grad = (attn_probs * (prob_grad - row_inner) * score_scale).astype(jnp.bfloat16)
    query_parts = jnp.einsum(
        "hqk,khd->qhd", score_grad, key_heads, preferred_element_type=jnp.float32
    )
    key_total = jnp.einsum(
        "hqk,qhd->khd", score_grad, query_heads, preferred_element_type=jnp.float32
    )
    value_total = jnp.einsum(
        "hqk,qhd->khd", probs_low, grad_heads, preferred_element_type=jnp.float32
    )
    query_grad = query_parts.reshape(seq_len, local_width)
    key_grad = key_total.reshape(seq_len, local_width)
    value_grad = value_total.reshape(seq_len, local_width)
    grad_query_bias = jnp.sum(query_grad, axis=0)
    grad_value_bias = jnp.sum(value_grad, axis=0)
    query_low = query_grad.astype(jnp.bfloat16)
    key_low = key_grad.astype(jnp.bfloat16)
    value_low = value_grad.astype(jnp.bfloat16)
    grad_query = matmul_tn(hidden_full, query_low)
    grad_key = matmul_tn(hidden_full, key_low)
    grad_value = matmul_tn(hidden_full, value_low)
    grad_in = (
        first_grad
        + lax.psum_scatter(
            (
                matmul_nt(query_low, query_full)
                + matmul_nt(key_low, key_full)
                + matmul_nt(value_low, value_full)
            ).astype(jnp.bfloat16),
            "tensor",
            scatter_dimension=0,
            tiled=True,
        ).astype(jnp.float32)
    ).astype(jnp.bfloat16)
    owned_rows = (
        lax.psum_scatter(grad_query, "dp", scatter_dimension=0, tiled=True),
        lax.psum_scatter(grad_key, "dp", scatter_dimension=0, tiled=True),
        lax.psum_scatter(grad_value, "dp", scatter_dimension=0, tiled=True),
        lax.psum_scatter(grad_up, "dp", scatter_dimension=0, tiled=True),
    )
    owned_cols = (
        lax.psum_scatter(grad_output, "dp", scatter_dimension=1, tiled=True),
        lax.psum_scatter(grad_down, "dp", scatter_dimension=1, tiled=True),
    )
    summed = lax.psum(
        (
            widen(grad_query_bias, tensor_index, n_tensor),
            widen(grad_value_bias, tensor_index, n_tensor),
            widen(grad_up_bias, tensor_index, n_tensor),
            grad_output_bias,
            grad_down_bias,
            grad_first_gain,
            grad_first_shift,
            grad_second_gain,
            grad_second_shift,
        ),
        ("dp", "tensor"),
    )
    local_ff = up_weight.shape[1]
    query_bias_grad = lax.dynamic_slice_in_dim(
        summed[0], tensor_index * local_width, local_width, 0
    )
    value_bias_grad = lax.dynamic_slice_in_dim(
        summed[1], tensor_index * local_width, local_width, 0
    )
    up_bias_grad = lax.dynamic_slice_in_dim(summed[2], tensor_index * local_ff, local_ff, 0)
    return (
        hidden_out,
        grad_in,
        owned_rows[0],
        owned_rows[1],
        owned_rows[2],
        owned_cols[0],
        owned_rows[3],
        owned_cols[1],
        query_bias_grad,
        value_bias_grad,
        summed[3],
        up_bias_grad,
        summed[4],
        summed[5],
        summed[6],
        summed[7],
        summed[8],
    )


def solution(mesh):
    in_specs = (
        P(("dp", "tensor"), None),
        P(("dp", "tensor"), None),
        P("dp"),
        P("dp", "tensor"),
        P("dp", "tensor"),
        P("dp", "tensor"),
        P("tensor", "dp"),
        P("dp", "tensor"),
        P("tensor", "dp"),
        P("tensor"),
        P("tensor"),
        P(),
        P("tensor"),
        P(),
        P(),
        P(),
        P(),
        P(),
    )
    out_specs = (
        P(("dp", "tensor"), None),
        P(("dp", "tensor"), None),
        P("dp", "tensor"),
        P("dp", "tensor"),
        P("dp", "tensor"),
        P("tensor", "dp"),
        P("dp", "tensor"),
        P("tensor", "dp"),
        P("tensor"),
        P("tensor"),
        P(),
        P("tensor"),
        P(),
        P(),
        P(),
        P(),
        P(),
    )
    return jax.shard_map(shards, mesh=mesh, in_specs=in_specs, out_specs=out_specs, check_vma=False)
```

profile of v0, /device:TPU:0, one launch (start us, length us, event | category | flops | bytes accessed | tf_op | source)
XLA Modules:
  0.0 855.3 jit_solution(8635387933695956339)
XLA Ops:
  9.5 33.4 %all_gather.32 = bf16[1024,256]{1,0:T(8,128)(2,1)S(1)} all-gather(bf16[128,256]{1,0:T(8,128)(2,1)} %param.21), channel_id=1, replica_groups=mesh['dp'=8,'tensor'=4] {'dp'}, dimensions={0}, use_global_device_ids=true | all-gather | bytes 589824 | tf_op jit(solution)/shard_map/all_gather | solution.py:58
  42.8 31.6 %all_gather.33 = bf16[1024,256]{1,0:T(8,128)(2,1)S(1)} all-gather(bf16[128,256]{1,0:T(8,128)(2,1)} %param.22), channel_id=1, replica_groups=mesh['dp'=8,'tensor'=4] {'dp'}, dimensions={0}, use_global_device_ids=true | all-gather | bytes 589824 | tf_op jit(solution)/shard_map/all_gather | solution.py:59
  74.5 31.8 %all_gather.31 = bf16[1024,256]{1,0:T(8,128)(2,1)S(1)} all-gather(bf16[128,256]{1,0:T(8,128)(2,1)} %param.23), channel_id=1, replica_groups=mesh['dp'=8,'tensor'=4] {'dp'}, dimensions={0}, use_global_device_ids=true | all-gather | bytes 589824 | tf_op jit(solution)/shard_map/all_gather | solution.py:60
  106.3 27.2 %all_gather.34 = bf16[256,1024]{1,0:T(8,128)(2,1)S(1)} all-gather(bf16[256,128]{1,0:T(8,128)(2,1)} %param.24), channel_id=1, replica_groups=mesh['dp'=8,'tensor'=4] {'dp'}, dimensions={1}, use_global_device_ids=true | all-gather | bytes 589824 | tf_op jit(solution)/shard_map/all_gather | solution.py:64
  133.5 1.9 convolution_convert_fusion.5
  143.8 23.5 %reduce-scatter.11.cloned.1.call-done = bf16[128,1024]{1,0:T(8,128)(2,1)} async-done(((bf16[512,1024]{1,0:T(8,128)(2,1)}), bf16[128,1024]{1,0:T(8,128)(2,1)}) %reduce-scatter.11.cloned.1.call-update) | async-done | bytes 262160 | tf_op jit(solution)/shard_map/reduce_scatter | solution.py:133
  172.1 21.9 %all-gather.11.cloned.1.call-done = bf16[1024,1024]{1,0:T(8,128)(2,1)} async-done(((bf16[128,1024]{1,0:T(8,128)(2,1)}), bf16[1024,1024]{1,0:T(8,128)(2,1)}) %all-gather.11.cloned.1.call-update) | async-done | bytes 2097168 | tf_op jit(solution)/shard_map/all_gather | solution.py:61
  194.0 17.2 %all-gather.9.cloned.1.call-done = bf16[512,1024]{1,0:T(8,128)(2,1)} async-done(((bf16[128,1024]{1,0:T(8,128)(2,1)}), bf16[512,1024]{1,0:T(8,128)(2,1)}) %all-gather.9.cloned.1.call-update) | async-done | bytes 1048592 | tf_op jit(solution)/shard_map/all_gather | solution.py:139
  211.2 4.9 multiply_convert_fusion.1
  216.1 47.5 %all-gather.13.cloned.1.call-done = bf16[1024,1024]{1,0:T(8,128)(2,1)} async-done(((bf16[1024,128]{1,0:T(8,128)(2,1)}), bf16[1024,1024]{1,0:T(8,128)(2,1)}) %all-gather.13.cloned.1.call-update) | async-done | bytes 2097168 | tf_op jit(solution)/shard_map/all_gather | solution.py:65
  263.6 4.3 convolution_convert_fusion.1
  267.9 23.1 %reduce-scatter.13.cloned.1.call-done = bf16[128,1024]{1,0:T(8,128)(2,1)} async-done(((bf16[512,1024]{1,0:T(8,128)(2,1)}), bf16[128,1024]{1,0:T(8,128)(2,1)}) %reduce-scatter.13.cloned.1.call-update) | async-done | bytes 262160 | tf_op jit(solution)/shard_map/reduce_scatter | solution.py:142
  294.1 16.6 %all-gather.15.cloned.1.call-done = bf16[512,1024]{1,0:T(8,128)(2,1)} async-done(((bf16[128,1024]{1,0:T(8,128)(2,1)}), bf16[512,1024]{1,0:T(8,128)(2,1)}) %all-gather.15.cloned.1.call-update) | async-done | bytes 1048592 | tf_op jit(solution)/shard_map/all_gather | solution.py:154
  310.7 4.6 fusion.53
  316.4 2.3 convolution_convert_fusion
  318.7 24.9 %reduce-scatter.15.cloned.1.call-done = bf16[128,1024]{1,0:T(8,128)(2,1)} async-done(((bf16[512,1024]{1,0:T(8,128)(2,1)}), bf16[128,1024]{1,0:T(8,128)(2,1)}) %reduce-scatter.15.cloned.1.call-update) | async-done | bytes 262160 | tf_op jit(solution)/shard_map/reduce_scatter | solution.py:160
  347.0 16.6 %all-gather.17.cloned.1.call-done = bf16[512,1024]{1,0:T(8,128)(2,1)} async-done(((bf16[128,1024]{1,0:T(8,128)(2,1)}), bf16[512,1024]{1,0:T(8,128)(2,1)}) %all-gather.17.cloned.1.call-update) | async-done | bytes 1048592 | tf_op jit(solution)/shard_map/all_gather | solution.py:168
  365.5 3.4 fusion.49
  370.5 2.7 fusion.54
  373.2 8.5 fusion.23
  383.2 9.1 %fusion.50 = (f32[4,64]{1,0:T(4,128)S(1)}, bf16[512,4,64]{0,2,1:T(8,128)(2,1)}) fusion(bf16[512,4,64]{0,2,1:T(8,128)(2,1)S(1)} %bitcast.71, f32[4,512,512]{1,2,0:T(8,128)} %fusion.54, f32[4,512]{1,0:T(4,128)S(1)} %log_add_fusion, f32[4,512,512]{1,2,0:T(8,128)} %copy-done.1, pred[512]{0:T(512)(128)(4,1)S(1)} %iota_compare_fusion), kind=kOutput, calls=%fused_computation.87 | convolution fusion | flops 146016512 | bytes 8922624 | tf_op jit(solution)/shard_map/hqk,khd->qhd/dot_general | solution.py:180
  392.3 2.5 convolution_bitcast_fusion.2
  399.6 2.8 fusion.57
  402.4 4.5 fusion.58
  408.2 3.3 fusion.35
  412.3 40.8 %all-reduce = (f32[1024]{0:T(1024)S(1)}, f32[1024]{0:T(1024)S(1)}, f32[1024]{0:T(1024)}, f32[4096]{0:T(1024)S(1)}, f32[1024]{0:T(1024)}, /*index=5*/f32[1024]{0:...) all-reduce(f32[1024]{0:T(1024)S(1)} %dynamic_update_slice.9, ...), channel_id=1, replica_groups=mesh['dp'=8,'tensor'=4] {'dp','tensor'}, use_global_device_ids=true, to_apply=%region_22.23 | all-reduce | flops 12288 | bytes 98304 | tf_op jit(solution)/shard_map/psum | solution.py:223
  456.6 45.8 %reduce-scatter.21.cloned.1.call-done = f32[128,256]{0,1:T(8,128)} async-done(((f32[1024,256]{0,1:T(8,128)}), f32[128,256]{0,1:T(8,128)}) %reduce-scatter.21.cloned.1.call-update) | async-done | bytes 131088 | tf_op jit(solution)/shard_map/reduce_scatter | solution.py:215
  504.1 65.3 %reduce-scatter.19.cloned.1.call-done = f32[128,256]{0,1:T(8,128)} async-done(((f32[1024,256]{0,1:T(8,128)}), f32[128,256]{0,1:T(8,128)}) %reduce-scatter.19.cloned.1.call-update) | async-done | bytes 131088 | tf_op jit(solution)/shard_map/reduce_scatter | solution.py:214
  571.1 24.5 %reduce-scatter.17.cloned.1.call-done = bf16[128,1024]{1,0:T(8,128)(2,1)} async-done(((bf16[512,1024]{1,0:T(8,128)(2,1)}), bf16[128,1024]{1,0:T(8,128)(2,1)}) %reduce-scatter.17.cloned.1.call-update) | async-done | bytes 262160 | tf_op jit(solution)/shard_map/reduce_scatter | solution.py:202
  597.3 66.8 %reduce-scatter.25.cloned.1.call-done = f32[256,128]{1,0:T(8,128)} async-done(((f32[256,1024]{1,0:T(8,128)}), f32[256,128]{1,0:T(8,128)}) %reduce-scatter.25.cloned.1.call-update) | async-done | bytes 131088 | tf_op jit(solution)/shard_map/reduce_scatter | solution.py:220
  664.1 91.9 %reduce-scatter.29.cloned.1.call-done = f32[1024,128]{1,0:T(8,128)} async-done(((f32[1024,1024]{1,0:T(8,128)}), f32[1024,128]{1,0:T(8,128)}) %reduce-scatter.29.cloned.1.call-update) | async-done | bytes 524304 | tf_op jit(solution)/shard_map/reduce_scatter | solution.py:221
  756.0 91.9 %reduce-scatter.27.cloned.1.call-done = f32[128,1024]{1,0:T(8,128)} async-done(((f32[1024,1024]{1,0:T(8,128)}), f32[128,1024]{1,0:T(8,128)}) %reduce-scatter.27.cloned.1.call-update) | async-done | bytes 524304 | tf_op jit(solution)/shard_map/reduce_scatter | solution.py:217
  (146 shorter events, 41.5 us)
Async XLA Ops:
  8.0 127.4 %copy-start.31 = (f32[256]{0:T(256)S(1)}, f32[256]{0:T(256)}, u32[]{:S(2)}) copy-start(f32[256]{0:T(256)} %param.27) | copy-start | bytes 3076
  8.0 125.5 %all-gather.7.cloned.1.call-start = ((), (), s32[]{:S(2)}) async-start(), calls=%async_computation.10 | async-start | bytes 1310720 | tf_op jit(solution)/shard_map/all_gather | solution.py:117
  8.8 158.6 %reduce-scatter.11.cloned.1.call-start = ((), (), s32[]{:S(2)}) async-start(), calls=%async_computation.11 | async-start | bytes 1310720 | tf_op jit(solution)/shard_map/reduce_scatter | solution.py:133
  42.8 94.4 %copy-start.7 = (bf16[1024,256]{1,0:T(8,128)(2,1)}, bf16[1024,256]{1,0:T(8,128)(2,1)S(1)}, u32[]{:S(2)}) copy-start(bf16[1024,256]{1,0:T(8,128)(2,1)S(1)} %all_gather.32) | copy-start | bytes 1572868
  106.3 33.7 %copy-start.4 = (bf16[1024,256]{1,0:T(8,128)(2,1)}, bf16[1024,256]{1,0:T(8,128)(2,1)S(1)}, u32[]{:S(2)}) copy-start(bf16[1024,256]{1,0:T(8,128)(2,1)S(1)} %all_gather.31) | copy-start | bytes 1572868
  133.5 8.1 copy-start.6
  140.5 26.8 %copy-start.2 = (bf16[128,1024]{1,0:T(8,128)(2,1)S(1)}, bf16[128,1024]{1,0:T(8,128)(2,1)}, u32[]{:S(2)}) copy-start(bf16[128,1024]{1,0:T(8,128)(2,1)} %param.18) | copy-start | bytes 786436
  140.5 26.8 %copy-start.23 = (f32[1024]{0:T(1024)S(1)}, f32[1024]{0:T(1024)}, u32[]{:S(2)}) copy-start(f32[1024]{0:T(1024)} %param.29) | copy-start | bytes 12292
  140.5 29.1 %copy-start.24 = (f32[1024]{0:T(1024)S(1)}, f32[1024]{0:T(1024)}, u32[]{:S(2)}) copy-start(f32[1024]{0:T(1024)} %param.32) | copy-start | bytes 12292
  140.5 29.1 %copy-start.25 = (f32[1024]{0:T(1024)S(1)}, f32[1024]{0:T(1024)}, u32[]{:S(2)}) copy-start(f32[1024]{0:T(1024)} %param.33) | copy-start | bytes 12292
  141.6 69.5 %copy-start.30 = (f32[1024]{0:T(1024)S(1)}, f32[1024]{0:T(1024)}, u32[]{:S(2)}) copy-start(f32[1024]{0:T(1024)} %param.30) | copy-start | bytes 12292
  143.2 50.8 %all-gather.11.cloned.1.call-start = ((), (), s32[]{:S(2)}) async-start(), calls=%async_computation.13 | async-start | bytes 2359296 | tf_op jit(solution)/shard_map/all_gather | solution.py:61
  143.7 67.4 %all-gather.9.cloned.1.call-start = ((), (), s32[]{:S(2)}) async-start(), calls=%async_computation.12 | async-start | bytes 1310720 | tf_op jit(solution)/shard_map/all_gather | solution.py:139
  171.5 92.1 %all-gather.13.cloned.1.call-start = ((), (), s32[]{:S(2)}) async-start(), calls=%async_computation.14 | async-start | bytes 2359296 | tf_op jit(solution)/shard_map/all_gather | solution.py:65
  172.1 118.9 %reduce-scatter.13.cloned.1.call-start = ((), (), s32[]{:S(2)}) async-start(), calls=%async_computation.15 | async-start | bytes 1310720 | tf_op jit(solution)/shard_map/reduce_scatter | solution.py:142
  216.1 74.9 %copy-start.3 = (bf16[128,1024]{1,0:T(8,128)(2,1)S(1)}, bf16[128,1024]{1,0:T(8,128)(2,1)}, u32[]{:S(2)}) copy-start(bf16[128,1024]{1,0:T(8,128)(2,1)} %reduce-scatter.11.cloned.1.call-done) | copy-start | bytes 786436
  216.1 74.9 %copy-start.27 = (f32[1024]{0:T(1024)S(1)}, f32[1024]{0:T(1024)}, u32[]{:S(2)}) copy-start(f32[1024]{0:T(1024)} %param.31) | copy-start | bytes 12292
  263.6 28.9 %copy-start.15 = (bf16[128,1024]{1,0:T(8,128)(2,1)S(1)}, bf16[128,1024]{1,0:T(8,128)(2,1)}, u32[]{:S(2)}) copy-start(bf16[128,1024]{1,0:T(8,128)(2,1)} %param.19) | copy-start | bytes 786436
  263.6 28.9 %copy-start.26 = (f32[1024]{0:T(1024)S(1)}, f32[1024]{0:T(1024)}, u32[]{:S(2)}) copy-start(f32[1024]{0:T(1024)} %param.34) | copy-start | bytes 12292
  263.6 29.2 %copy-start.28 = (f32[1024]{0:T(1024)S(1)}, f32[1024]{0:T(1024)}, u32[]{:S(2)}) copy-start(f32[1024]{0:T(1024)} %param.35) | copy-start | bytes 12292
  267.8 42.9 %all-gather.15.cloned.1.call-start = ((), (), s32[]{:S(2)}) async-start(), calls=%async_computation.16 | async-start | bytes 1310720 | tf_op jit(solution)/shard_map/all_gather | solution.py:154
  293.9 49.7 %reduce-scatter.15.cloned.1.call-start = ((), (), s32[]{:S(2)}) async-start(), calls=%async_computation.17 | async-start | bytes 1310720 | tf_op jit(solution)/shard_map/reduce_scatter | solution.py:160
  318.7 45.0 %all-gather.17.cloned.1.call-start = ((), (), s32[]{:S(2)}) async-start(), calls=%async_computation.18 | async-start | bytes 1310720 | tf_op jit(solution)/shard_map/all_gather | solution.py:168
  347.0 108.0 %reduce-scatter.23.cloned.1.call-start = ((), (), s32[]{:S(2)}) async-start(), calls=%async_computation.22 | async-start | bytes 1179648 | tf_op jit(solution)/shard_map/reduce_scatter | solution.py:216
  370.4 132.1 %reduce-scatter.21.cloned.1.call-start = ((), (), s32[]{:S(2)}) async-start(), calls=%async_computation.21 | async-start | bytes 1179648 | tf_op jit(solution)/shard_map/reduce_scatter | solution.py:215
  373.2 10.0 %copy-start.12 = (bf16[512,256]{0,1:T(8,128)(2,1)S(1)}, bf16[512,256]{0,1:T(8,128)(2,1)}, u32[]{:S(2)}) copy-start(bf16[512,256]{0,1:T(8,128)(2,1)} %copy-done.11) | copy-start | bytes 786436
  381.7 10.6 %copy-start.16 = (bf16[4,64,512]{2,1,0:T(8,128)(2,1)}, bf16[4,64,512]{2,1,0:T(8,128)(2,1)S(1)}, u32[]{:S(2)}) copy-start(bf16[4,64,512]{2,1,0:T(8,128)(2,1)S(1)} %fusion.23) | copy-start | bytes 786436
  383.1 186.3 %reduce-scatter.19.cloned.1.call-start = ((), (), s32[]{:S(2)}) async-start(), calls=%async_computation.20 | async-start | bytes 1179648 | tf_op jit(solution)/shard_map/reduce_scatter | solution.py:214
  394.8 200.8 %reduce-scatter.17.cloned.1.call-start = ((), (), s32[]{:S(2)}) async-start(), calls=%async_computation.19 | async-start | bytes 1310720 | tf_op jit(solution)/shard_map/reduce_scatter | solution.py:202
  399.5 264.6 %reduce-scatter.25.cloned.1.call-start = ((), (), s32[]{:S(2)}) async-start(), calls=%async_computation.23 | async-start | bytes 1179648 | tf_op jit(solution)/shard_map/reduce_scatter | solution.py:220
  402.4 353.6 %reduce-scatter.29.cloned.1.call-start = ((), (), s32[]{:S(2)}) async-start(), calls=%async_computation.25 | async-start | bytes 4718592 | tf_op jit(solution)/shard_map/reduce_scatter | solution.py:221
  407.0 440.9 %reduce-scatter.27.cloned.1.call-start = ((), (), s32[]{:S(2)}) async-start(), calls=%async_computation.24 | async-start | bytes 4718592 | tf_op jit(solution)/shard_map/reduce_scatter | solution.py:217
  (17 other events, 53.9 us)
Sparse Core Ops, SparseCore 0:
  10.4 19.4 all-gather.6
  143.3 24.0 reduce-scatter.10
  268.0 22.9 reduce-scatter.12
  294.0 16.6 all-gather.14
  318.8 24.7 reduce-scatter.14
Sparse Core Ops, SparseCore 1:
  145.8 48.2 all-gather.10
  196.0 15.1 all-gather.8
  213.1 50.4 all-gather.12
  347.0 16.5 all-gather.16
  370.5 64.9 reduce-scatter.22
  438.8 63.6 reduce-scatter.20
  505.7 63.6 reduce-scatter.18
  571.8 23.7 reduce-scatter.16
  599.4 64.6 reduce-scatter.24
  668.4 87.6 reduce-scatter.28
  760.1 87.8 reduce-scatter.26
where the time goes:
time: 856 us; the launch traced here: 855 us
  waiting for transfers between devices  580 us (68%)
  blocking collectives  165 us (19%)
  matrix products  69.6 us (8%)
  between operations  16.7 us (2%)
  other arithmetic  12.9 us (2%)
  local copies, waits for them, and re-layouts  10.7 us (1%)
    reduce_scatter x1, waiting for transfers between devices, shards(): lax.psum_scatter(grad_up, 'dp', scatter_dimension=0, tiled=True)  91.9 us
    reduce_scatter x1, waiting for transfers between devices, shards(): lax.psum_scatter(grad_down, 'dp', scatter_dimension=1, tiled=True)  91.9 us
    reduce_scatter x1, waiting for transfers between devices, shards(): lax.psum_scatter(grad_output, 'dp', scatter_dimension=1, tiled=True)  66.8 us
    reduce_scatter x1, waiting for transfers between devices, shards(): lax.psum_scatter(grad_query, 'dp', scatter_dimension=0, tiled=True)  65.3 us
    all_gather x1, waiting for transfers between devices, fetch_weights(): lax.all_gather(down_weight, 'dp', axis=1, tiled=True)  47.5 us
    reduce_scatter x1, waiting for transfers between devices, shards(): lax.psum_scatter(grad_key, 'dp', scatter_dimension=0, tiled=True)  45.8 us
    psum x1, blocking collectives, shards(): lax.psum((widen(grad_query_bias, tensor_index, n_tensor), widen(grad_valu...  40.8 us
    all_gather x1, blocking collectives, fetch_weights(): lax.all_gather(query_weight, 'dp', axis=0, tiled=True)  33.4 us
  transfers between devices with their start and end apart: 16, of which 14 were waited for; matrix products, arithmetic and copies ran while one was open for 7% of the time, Pallas kernels for 0%

commit v1 on v0

--- a/solution.py
+++ b/solution.py
@@ -1,3 +1,4 @@
+import functools
 import jax
 import jax.numpy as jnp
 from jax import lax
@@ -8,6 +9,22 @@
 ROOT_HALF = 0.7071067811865476
 INV_ROOT_TWO_PI = 0.3989422804014327
 MASKED = -1e30
+
+
+def numbers_connect(frame, lane_axis):
+    r_now, block_last, k_now = (lax.axis_size(lane_axis), lax.axis_index(lane_axis), frame.shape[1])
+    buffers = [(jj, (jj + 1) % r_now) for jj in range(r_now)]
+    item_now = jnp.zeros((*frame.shape[:1], r_now * k_now, *frame.shape[2:]), frame.dtype)
+    seen_now = frame
+    for dev_j in range(r_now):
+        opened = (block_last - dev_j) % r_now
+        item_now = lax.dynamic_update_slice_in_dim(item_now, seen_now, opened * k_now, axis=1)
+        if dev_j < r_now - 1:
+            seen_now = lax.ppermute(seen_now, lane_axis, buffers)
+    return item_now
+
+
+return_all_windows = functools.partial(numbers_connect, lane_axis="dp")
 
 
 def matmul(left_side, right_side):
@@ -62,7 +79,7 @@
     )
     col_parts = (
         lax.all_gather(output_weight, "dp", axis=1, tiled=True),
-        lax.all_gather(down_weight, "dp", axis=1, tiled=True),
+        return_all_windows(down_weight),
     )
     return (row_parts, col_parts)
 

time: 856 us -> 827 us (0.966)
  waiting for transfers between devices: 580 us -> 540 us
  local copies, waits for them, and re-layouts: 10.7 us -> 20.3 us
    ppermute x0 -> x7, waiting for transfers between devices: none -> 71 us  [numbers_connect(): seen_now = lax.ppermute(seen_now, lane_axis, buffers)]
    all_gather x1 -> x0, waiting for transfers between devices: 47.5 us -> none  [fetch_weights(): lax.all_gather(down_weight, 'dp', axis=1, tiled=True)]
    reduce_scatter x1, waiting for transfers between devices: 23.5 us -> 0.01 us  [shards(): lax.psum_scatter(matmul(context, output_full).astype(jnp.bfloat16), 'tens...]
    all_gather x1, waiting for transfers between devices: 21.9 us -> 0.01 us  [fetch_weights(): lax.all_gather(up_weight, 'dp', axis=0, tiled=True)]
    all_gather x1, waiting for transfers between devices: 17.2 us -> 0.01 us  [shards(): normed_full = lax.all_gather(first_low, 'tensor', axis=0, tiled=True)]
  transfers between devices with their start and end apart: 16 -> 22, of which waited for: 14 -> 17; matrix products, arithmetic and copies ran while one was open for 7% -> 7% of each run, Pallas kernels for 0% -> 0%
where the time goes in v1:
time: 827 us; the launch traced here: 826 us
  waiting for transfers between devices  540 us (65%)
  blocking collectives  165 us (20%)
  matrix products  67.5 us (8%)
  local copies, waits for them, and re-layouts  20.3 us (2%)
  between operations  16.7 us (2%)
  other arithmetic  12.9 us (2%)
    reduce_scatter x1, waiting for transfers between devices, shards(): lax.psum_scatter(grad_down, 'dp', scatter_dimension=1, tiled=True)  91.9 us
    reduce_scatter x1, waiting for transfers between devices, shards(): lax.psum_scatter(grad_up, 'dp', scatter_dimension=0, tiled=True)  91.9 us
    ppermute x7, waiting for transfers between devices, numbers_connect(): seen_now = lax.ppermute(seen_now, lane_axis, buffers)  71 us
    reduce_scatter x1, waiting for transfers between devices, shards(): lax.psum_scatter(grad_output, 'dp', scatter_dimension=1, tiled=True)  66.9 us
    reduce_scatter x1, waiting for transfers between devices, shards(): lax.psum_scatter(grad_query, 'dp', scatter_dimension=0, tiled=True)  65.4 us
    reduce_scatter x1, waiting for transfers between devices, shards(): lax.psum_scatter(grad_key, 'dp', scatter_dimension=0, tiled=True)  47.2 us
    psum x1, blocking collectives, shards(): lax.psum((widen(grad_query_bias, tensor_index, n_tensor), widen(grad_valu...  40.9 us
    all_gather x1, blocking collectives, fetch_weights(): lax.all_gather(query_weight, 'dp', axis=0, tiled=True)  33.4 us
  transfers between devices with their start and end apart: 22, of which 17 were waited for; matrix products, arithmetic and copies ran while one was open for 7% of the time, Pallas kernels for 0%

profile of v1, /device:TPU:0, one launch (start us, length us, event | category | flops | bytes accessed | tf_op | source)
XLA Modules:
  0.0 826.1 jit_solution(3894954953680938913)
XLA Ops:
  9.5 33.4 %all_gather.29 = bf16[1024,256]{1,0:T(8,128)(2,1)S(1)} all-gather(bf16[128,256]{1,0:T(8,128)(2,1)} %param.21), channel_id=1, replica_groups=mesh['dp'=8,'tensor'=4] {'dp'}, dimensions={0}, use_global_device_ids=true | all-gather | bytes 589824 | tf_op jit(solution)/shard_map/all_gather | solution.py:75
  42.8 31.6 %all_gather.30 = bf16[1024,256]{1,0:T(8,128)(2,1)S(1)} all-gather(bf16[128,256]{1,0:T(8,128)(2,1)} %param.22), channel_id=1, replica_groups=mesh['dp'=8,'tensor'=4] {'dp'}, dimensions={0}, use_global_device_ids=true | all-gather | bytes 589824 | tf_op jit(solution)/shard_map/all_gather | solution.py:76
  74.5 31.8 %all_gather.28 = bf16[1024,256]{1,0:T(8,128)(2,1)S(1)} all-gather(bf16[128,256]{1,0:T(8,128)(2,1)} %param.23), channel_id=1, replica_groups=mesh['dp'=8,'tensor'=4] {'dp'}, dimensions={0}, use_global_device_ids=true | all-gather | bytes 589824 | tf_op jit(solution)/shard_map/all_gather | solution.py:77
  106.3 27.2 %all_gather.31 = bf16[256,1024]{1,0:T(8,128)(2,1)S(1)} all-gather(bf16[256,128]{1,0:T(8,128)(2,1)} %param.24), channel_id=1, replica_groups=mesh['dp'=8,'tensor'=4] {'dp'}, dimensions={1}, use_global_device_ids=true | all-gather | bytes 589824 | tf_op jit(solution)/shard_map/all_gather | solution.py:81
  146.0 6.9 collective-permute-done
  152.9 14.5 %collective-permute-done.1 = bf16[1024,128]{1,0:T(8,128)(2,1)S(1)} collective-permute-done((bf16[1024,128]{1,0:T(8,128)(2,1)S(1)}, bf16[1024,128]{1,0:T(8,128)(2,1)S(1)}, u32[]{:S(2)}, u32[]{:S(2)}) %collective-permute-start.1) | collective-permute-done | bytes 262176 | tf_op jit(solution)/shard_map/ppermute | solution.py:23
  171.5 4.9 collective-permute-done.2
  176.4 16.7 %collective-permute-done.3 = bf16[1024,128]{1,0:T(8,128)(2,1)S(1)} collective-permute-done((bf16[1024,128]{1,0:T(8,128)(2,1)S(1)}, bf16[1024,128]{1,0:T(8,128)(2,1)S(1)}, u32[]{:S(2)}, u32[]{:S(2)}) %collective-permute-start.3) | collective-permute-done | bytes 262176 | tf_op jit(solution)/shard_map/ppermute | solution.py:23
  195.5 13.2 %collective-permute-done.4 = bf16[1024,128]{1,0:T(8,128)(2,1)} collective-permute-done((bf16[1024,128]{1,0:T(8,128)(2,1)S(1)}, bf16[1024,128]{1,0:T(8,128)(2,1)}, u32[]{:S(2)}, u32[]{:S(2)}) %collective-permute-start.4) | collective-permute-done | bytes 262176 | tf_op jit(solution)/shard_map/ppermute | solution.py:23
  211.0 9.1 %collective-permute-done.5 = bf16[1024,128]{1,0:T(8,128)(2,1)S(1)} collective-permute-done((bf16[1024,128]{1,0:T(8,128)(2,1)}, bf16[1024,128]{1,0:T(8,128)(2,1)S(1)}, u32[]{:S(2)}, u32[]{:S(2)}) %collective-permute-start.5) | collective-permute-done | bytes 262176 | tf_op jit(solution)/shard_map/ppermute | solution.py:23
  223.3 5.8 collective-permute-done.6
  229.8 4.6 multiply_convert_fusion.1
  235.4 3.9 convolution_convert_fusion.1
  239.5 22.3 %reduce-scatter.13.cloned.1.call-done = bf16[128,1024]{1,0:T(8,128)(2,1)} async-done(((bf16[512,1024]{1,0:T(8,128)(2,1)}), bf16[128,1024]{1,0:T(8,128)(2,1)}) %reduce-scatter.13.cloned.1.call-update) | async-done | bytes 262160 | tf_op jit(solution)/shard_map/reduce_scatter | solution.py:159
  264.9 16.4 %all-gather.12.cloned.1.call-done = bf16[512,1024]{1,0:T(8,128)(2,1)} async-done(((bf16[128,1024]{1,0:T(8,128)(2,1)}), bf16[512,1024]{1,0:T(8,128)(2,1)}) %all-gather.12.cloned.1.call-update) | async-done | bytes 1048592 | tf_op jit(solution)/shard_map/all_gather | solution.py:171
  281.4 4.6 fusion.53
  289.3 24.9 %reduce-scatter.15.cloned.1.call-done = bf16[128,1024]{1,0:T(8,128)(2,1)} async-done(((bf16[512,1024]{1,0:T(8,128)(2,1)}), bf16[128,1024]{1,0:T(8,128)(2,1)}) %reduce-scatter.15.cloned.1.call-update) | async-done | bytes 262160 | tf_op jit(solution)/shard_map/reduce_scatter | solution.py:177
  317.6 16.6 %all-gather.14.cloned.1.call-done = bf16[512,1024]{1,0:T(8,128)(2,1)} async-done(((bf16[128,1024]{1,0:T(8,128)(2,1)}), bf16[512,1024]{1,0:T(8,128)(2,1)}) %all-gather.14.cloned.1.call-update) | async-done | bytes 1048592 | tf_op jit(solution)/shard_map/all_gather | solution.py:185
  336.1 3.4 fusion.49
  341.0 2.7 fusion.54
  343.8 8.5 %fusion.23 = bf16[4,64,512]{2,1,0:T(8,128)(2,1)S(1)} fusion(bf16[512,4,64]{0,2,1:T(8,128)(2,1)S(1)} %bitcast.79, f32[4,512,512]{1,2,0:T(8,128)} %fusion.54, f32[4,512,512]{1,2,0:T(8,128)} %copy-done.1, f32[4,512]{1,0:T(4,128)S(1)} %log_add_fusion, pred[512]{0:T(512)(128)(4,1)S(1)} %iota_compare_fusion), kind=kOutput, calls=%fused_computation.33 | convolution fusion | flops 145885696 | bytes 8921600 | tf_op jit(solution)/shard_map/hqk,qhd->khd/dot_general | solution.py:200
  353.8 9.1 %fusion.50 = (f32[4,64]{1,0:T(4,128)S(1)}, bf16[512,4,64]{0,2,1:T(8,128)(2,1)}) fusion(bf16[512,4,64]{0,2,1:T(8,128)(2,1)S(1)} %bitcast.71, f32[4,512,512]{1,2,0:T(8,128)} %fusion.54, f32[4,512]{1,0:T(4,128)S(1)} %log_add_fusion, f32[4,512,512]{1,2,0:T(8,128)} %copy-done.1, pred[512]{0:T(512)(128)(4,1)S(1)} %iota_compare_fusion), kind=kOutput, calls=%fused_computation.95 | convolution fusion | flops 146016512 | bytes 8922624 | tf_op jit(solution)/shard_map/hqk,khd->qhd/dot_general | solution.py:197
  362.8 2.5 convolution_bitcast_fusion.2
  371.7 4.5 fusion.58
  377.4 3.3 fusion.35
  381.6 40.9 %all-reduce = (f32[1024]{0:T(1024)S(1)}, f32[1024]{0:T(1024)S(1)}, f32[1024]{0:T(1024)}, f32[4096]{0:T(1024)S(1)}, f32[1024]{0:T(1024)}, /*index=5*/f32[1024]{0:...) all-reduce(f32[1024]{0:T(1024)S(1)} %dynamic_update_slice.41, ...), channel_id=1, replica_groups=mesh['dp'=8,'tensor'=4] {'dp','tensor'}, use_global_device_ids=true, to_apply=%region_22.23 | all-reduce | flops 12288 | bytes 98304 | tf_op jit(solution)/shard_map/psum | solution.py:240
  426.0 47.2 %reduce-scatter.21.cloned.1.call-done = f32[128,256]{0,1:T(8,128)} async-done(((f32[1024,256]{0,1:T(8,128)}), f32[128,256]{0,1:T(8,128)}) %reduce-scatter.21.cloned.1.call-update) | async-done | bytes 131088 | tf_op jit(solution)/shard_map/reduce_scatter | solution.py:232
  474.8 65.4 %reduce-scatter.19.cloned.1.call-done = f32[128,256]{0,1:T(8,128)} async-done(((f32[1024,256]{0,1:T(8,128)}), f32[128,256]{0,1:T(8,128)}) %reduce-scatter.19.cloned.1.call-update) | async-done | bytes 131088 | tf_op jit(solution)/shard_map/reduce_scatter | solution.py:231
  541.8 24.5 %reduce-scatter.17.cloned.1.call-done = bf16[128,1024]{1,0:T(8,128)(2,1)} async-done(((bf16[512,1024]{1,0:T(8,128)(2,1)}), bf16[128,1024]{1,0:T(8,128)(2,1)}) %reduce-scatter.17.cloned.1.call-update) | async-done | bytes 262160 | tf_op jit(solution)/shard_map/reduce_scatter | solution.py:219
  568.1 66.9 %reduce-scatter.25.cloned.1.call-done = f32[256,128]{1,0:T(8,128)} async-done(((f32[256,1024]{1,0:T(8,128)}), f32[256,128]{1,0:T(8,128)}) %reduce-scatter.25.cloned.1.call-update) | async-done | bytes 131088 | tf_op jit(solution)/shard_map/reduce_scatter | solution.py:237
  634.9 91.9 %reduce-scatter.29.cloned.1.call-done = f32[1024,128]{1,0:T(8,128)} async-done(((f32[1024,1024]{1,0:T(8,128)}), f32[1024,128]{1,0:T(8,128)}) %reduce-scatter.29.cloned.1.call-update) | async-done | bytes 524304 | tf_op jit(solution)/shard_map/reduce_scatter | solution.py:238
  726.9 91.9 %reduce-scatter.27.cloned.1.call-done = f32[128,1024]{1,0:T(8,128)} async-done(((f32[1024,1024]{1,0:T(8,128)}), f32[128,1024]{1,0:T(8,128)}) %reduce-scatter.27.cloned.1.call-update) | async-done | bytes 524304 | tf_op jit(solution)/shard_map/reduce_scatter | solution.py:234
  (168 shorter events, 58.3 us)
Async XLA Ops:
  8.0 127.4 %copy-start.32 = (f32[256]{0:T(256)S(1)}, f32[256]{0:T(256)}, u32[]{:S(2)}) copy-start(f32[256]{0:T(256)} %param.27) | copy-start | bytes 3076
  8.0 125.5 %all-gather.6.cloned.1.call-start = ((), (), s32[]{:S(2)}) async-start(), calls=%async_computation.10 | async-start | bytes 1310720 | tf_op jit(solution)/shard_map/all_gather | solution.py:134
  8.8 158.6 %reduce-scatter.11.cloned.1.call-start = ((), (), s32[]{:S(2)}) async-start(), calls=%async_computation.11 | async-start | bytes 1310720 | tf_op jit(solution)/shard_map/reduce_scatter | solution.py:150
  42.8 94.3 %copy-start.7 = (bf16[1024,256]{1,0:T(8,128)(2,1)}, bf16[1024,256]{1,0:T(8,128)(2,1)S(1)}, u32[]{:S(2)}) copy-start(bf16[1024,256]{1,0:T(8,128)(2,1)S(1)} %all_gather.29) | copy-start | bytes 1572868
  106.3 32.9 %copy-start.4 = (bf16[1024,256]{1,0:T(8,128)(2,1)}, bf16[1024,256]{1,0:T(8,128)(2,1)S(1)}, u32[]{:S(2)}) copy-start(bf16[1024,256]{1,0:T(8,128)(2,1)S(1)} %all_gather.28) | copy-start | bytes 1572868
  139.7 27.6 %copy-start.2 = (bf16[128,1024]{1,0:T(8,128)(2,1)S(1)}, bf16[128,1024]{1,0:T(8,128)(2,1)}, u32[]{:S(2)}) copy-start(bf16[128,1024]{1,0:T(8,128)(2,1)} %param.18) | copy-start | bytes 786436
  139.8 29.9 %copy-start.25 = (f32[1024]{0:T(1024)S(1)}, f32[1024]{0:T(1024)}, u32[]{:S(2)}) copy-start(f32[1024]{0:T(1024)} %param.32) | copy-start | bytes 12292
  139.8 29.9 %copy-start.26 = (f32[1024]{0:T(1024)S(1)}, f32[1024]{0:T(1024)}, u32[]{:S(2)}) copy-start(f32[1024]{0:T(1024)} %param.33) | copy-start | bytes 12292
  143.1 86.7 %all-gather.10.cloned.1.call-start = ((), (), s32[]{:S(2)}) async-start(), calls=%async_computation.13 | async-start | bytes 2359296 | tf_op jit(solution)/shard_map/all_gather | solution.py:78
  143.7 86.2 %all-gather.8.cloned.1.call-start = ((), (), s32[]{:S(2)}) async-start(), calls=%async_computation.12 | async-start | bytes 1310720 | tf_op jit(solution)/shard_map/all_gather | solution.py:156
  143.7 9.1 %collective-permute-start = (bf16[1024,128]{1,0:T(8,128)(2,1)S(1)}, bf16[1024,128]{1,0:T(8,128)(2,1)S(1)}, u32[]{:S(2)}, u32[]{:S(2)}) collective-permute-start(bf16[1024,128]{1,0:T(8,128)(2,1)S(1)} %copy-done.23), channel_id=1, source_target_pairs={{0,4},{4,8},{8,12},{12,16},{16,20},{20,24},{24,28},{28,0},{1,5},{5... | collective-permute-start | bytes 786440 | tf_op jit(solution)/shard_map/ppermute | solution.py:23
  152.9 14.5 %collective-permute-start.1 = (bf16[1024,128]{1,0:T(8,128)(2,1)S(1)}, bf16[1024,128]{1,0:T(8,128)(2,1)S(1)}, u32[]{:S(2)}, u32[]{:S(2)}) collective-permute-start(bf16[1024,128]{1,0:T(8,128)(2,1)S(1)} %collective-permute-done), channel_id=1, source_target_pairs={{0,4},{4,8},{8,12},{12,16},{16,20},{20,24},{24,28},{28,0},{1,5},{5... | collective-permute-start | bytes 786440 | tf_op jit(solution)/shard_map/ppermute | solution.py:23
  167.3 9.1 %collective-permute-start.2 = (bf16[1024,128]{1,0:T(8,128)(2,1)S(1)}, bf16[1024,128]{1,0:T(8,128)(2,1)S(1)}, u32[]{:S(2)}, u32[]{:S(2)}) collective-permute-start(bf16[1024,128]{1,0:T(8,128)(2,1)S(1)} %collective-permute-done.1), channel_id=1, source_target_pairs={{0,4},{4,8},{8,12},{12,16},{16,20},{20,24},{24,28},{28,0},{1,5},{5... | collective-permute-start | bytes 786440 | tf_op jit(solution)/shard_map/ppermute | solution.py:23
  168.5 61.4 %copy-start.31 = (f32[1024]{0:T(1024)S(1)}, f32[1024]{0:T(1024)}, u32[]{:S(2)}) copy-start(f32[1024]{0:T(1024)} %param.30) | copy-start | bytes 12292
  171.5 90.3 %reduce-scatter.13.cloned.1.call-start = ((), (), s32[]{:S(2)}) async-start(), calls=%async_computation.14 | async-start | bytes 1310720 | tf_op jit(solution)/shard_map/reduce_scatter | solution.py:159
  176.4 16.7 %collective-permute-start.3 = (bf16[1024,128]{1,0:T(8,128)(2,1)S(1)}, bf16[1024,128]{1,0:T(8,128)(2,1)S(1)}, u32[]{:S(2)}, u32[]{:S(2)}) collective-permute-start(bf16[1024,128]{1,0:T(8,128)(2,1)S(1)} %collective-permute-done.2), channel_id=1, source_target_pairs={{0,4},{4,8},{8,12},{12,16},{16,20},{20,24},{24,28},{28,0},{1,5},{5... | collective-permute-start | bytes 786440 | tf_op jit(solution)/shard_map/ppermute | solution.py:23
  193.1 15.6 %collective-permute-start.4 = (bf16[1024,128]{1,0:T(8,128)(2,1)S(1)}, bf16[1024,128]{1,0:T(8,128)(2,1)}, u32[]{:S(2)}, u32[]{:S(2)}) collective-permute-start(bf16[1024,128]{1,0:T(8,128)(2,1)S(1)} %collective-permute-done.3), channel_id=1, source_target_pairs={{0,4},{4,8},{8,12},{12,16},{16,20},{20,24},{24,28},{28,0},{1,5},{5... | collective-permute-start | bytes 786440 | tf_op jit(solution)/shard_map/ppermute | solution.py:23
  208.7 11.3 %collective-permute-start.5 = (bf16[1024,128]{1,0:T(8,128)(2,1)}, bf16[1024,128]{1,0:T(8,128)(2,1)S(1)}, u32[]{:S(2)}, u32[]{:S(2)}) collective-permute-start(bf16[1024,128]{1,0:T(8,128)(2,1)} %collective-permute-done.4), channel_id=1, source_target_pairs={{0,4},{4,8},{8,12},{12,16},{16,20},{20,24},{24,28},{28,0},{1,5},{5... | collective-permute-start | bytes 786440 | tf_op jit(solution)/shard_map/ppermute | solution.py:23
  220.0 9.1 %collective-permute-start.6 = (bf16[1024,128]{1,0:T(8,128)(2,1)S(1)}, bf16[1024,128]{1,0:T(8,128)(2,1)S(1)}, u32[]{:S(2)}, u32[]{:S(2)}) collective-permute-start(bf16[1024,128]{1,0:T(8,128)(2,1)S(1)} %collective-permute-done.5), channel_id=1, source_target_pairs={{0,4},{4,8},{8,12},{12,16},{16,20},{20,24},{24,28},{28,0},{1,5},{5... | collective-permute-start | bytes 786440 | tf_op jit(solution)/shard_map/ppermute | solution.py:23
  235.4 27.9 %copy-start.15 = (bf16[128,1024]{1,0:T(8,128)(2,1)S(1)}, bf16[128,1024]{1,0:T(8,128)(2,1)}, u32[]{:S(2)}) copy-start(bf16[128,1024]{1,0:T(8,128)(2,1)} %param.19) | copy-start | bytes 786436
  235.4 27.9 %copy-start.27 = (f32[1024]{0:T(1024)S(1)}, f32[1024]{0:T(1024)}, u32[]{:S(2)}) copy-start(f32[1024]{0:T(1024)} %param.34) | copy-start | bytes 12292
  235.4 28.2 %copy-start.29 = (f32[1024]{0:T(1024)S(1)}, f32[1024]{0:T(1024)}, u32[]{:S(2)}) copy-start(f32[1024]{0:T(1024)} %param.35) | copy-start | bytes 12292
  239.4 42.0 %all-gather.12.cloned.1.call-start = ((), (), s32[]{:S(2)}) async-start(), calls=%async_computation.15 | async-start | bytes 1310720 | tf_op jit(solution)/shard_map/all_gather | solution.py:171
  264.7 49.5 %reduce-scatter.15.cloned.1.call-start = ((), (), s32[]{:S(2)}) async-start(), calls=%async_computation.16 | async-start | bytes 1310720 | tf_op jit(solution)/shard_map/reduce_scatter | solution.py:177
  289.3 45.0 %all-gather.14.cloned.1.call-start = ((), (), s32[]{:S(2)}) async-start(), calls=%async_computation.17 | async-start | bytes 1310720 | tf_op jit(solution)/shard_map/all_gather | solution.py:185
  317.6 106.7 %reduce-scatter.23.cloned.1.call-start = ((), (), s32[]{:S(2)}) async-start(), calls=%async_computation.21 | async-start | bytes 1179648 | tf_op jit(solution)/shard_map/reduce_scatter | solution.py:233
  341.0 132.2 %reduce-scatter.21.cloned.1.call-start = ((), (), s32[]{:S(2)}) async-start(), calls=%async_computation.20 | async-start | bytes 1179648 | tf_op jit(solution)/shard_map/reduce_scatter | solution.py:232
  353.7 186.5 %reduce-scatter.19.cloned.1.call-start = ((), (), s32[]{:S(2)}) async-start(), calls=%async_computation.19 | async-start | bytes 1179648 | tf_op jit(solution)/shard_map/reduce_scatter | solution.py:231
  365.3 201.0 %reduce-scatter.17.cloned.1.call-start = ((), (), s32[]{:S(2)}) async-start(), calls=%async_computation.18 | async-start | bytes 1310720 | tf_op jit(solution)/shard_map/reduce_scatter | solution.py:219
  370.1 264.9 %reduce-scatter.25.cloned.1.call-start = ((), (), s32[]{:S(2)}) async-start(), calls=%async_computation.22 | async-start | bytes 1179648 | tf_op jit(solution)/shard_map/reduce_scatter | solution.py:237
  371.6 355.3 %reduce-scatter.29.cloned.1.call-start = ((), (), s32[]{:S(2)}) async-start(), calls=%async_computation.24 | async-start | bytes 4718592 | tf_op jit(solution)/shard_map/reduce_scatter | solution.py:238
  376.2 442.5 %reduce-scatter.27.cloned.1.call-start = ((), (), s32[]{:S(2)}) async-start(), calls=%async_computation.23 | async-start | bytes 4718592 | tf_op jit(solution)/shard_map/reduce_scatter | solution.py:234
  (24 other events, 154.5 us)
Sparse Core Ops, SparseCore 0:
  10.4 19.4 all-gather.5
  143.2 24.0 reduce-scatter.10
  239.5 22.2 reduce-scatter.12
  289.4 24.7 reduce-scatter.14
Sparse Core Ops, SparseCore 1:
  145.7 58.0 all-gather.9
  205.8 19.6 all-gather.7
  264.8 16.5 all-gather.11
  317.7 16.5 all-gather.13
  341.1 64.8 reduce-scatter.22
  409.4 63.7 reduce-scatter.20
  476.4 63.7 reduce-scatter.18
  542.6 23.7 reduce-scatter.16
  570.2 64.7 reduce-scatter.24
  639.2 87.6 reduce-scatter.28
  730.9 87.8 reduce-scatter.26
